TPU v7x, 512 devices: a whole 4x8x8 slice. The times are simulated.
512 devices in a mesh: ctx: 32 (over y, z_lo), head: 4 (over x), batch: 4 (over z_hi, core).
Axes of the slice: x: 4, y: 8, z: 8 (z_hi: 2, z_lo: 4; z = z_hi * 4 + z_lo), core: 2. Of those that a mesh axis runs over, the one named last changes fastest.
Arguments:
- queries: bfloat16 [4, 4096, 20, 128], P('batch', 'ctx', 'head'), may hold values from -64 to 64
- key_rows: bfloat16 [4, 4096, 4, 128], P('batch', 'ctx', 'head'), may hold values from -8 to 8
- block_order: int32 [64], replicated, may hold values from 0 to 63, each once
- conv_len: int32 [4], replicated, may hold values from 2048 to 4096
- gate_wq: float32 [128, 128], replicated, may hold values from -32 to 32
- gate_wk: float32 [384, 128], replicated, may hold values from -32 to 32
Outputs:
- teacher_map: float32 [4, 20, 64, 64], P('batch', 'head', 'ctx')
- grad_wq: float32 [128, 128], replicated
- grad_wk: float32 [384, 128], replicated
All inputs are finite; a program needn't handle non-finite values.
Results may differ from a plain program's by a relative error of at most 0.0003.
Values may be sent and summed in bfloat16 or wider, within the bound.
No kernel may reach another device: no remote copies, remote signals or barrier semaphores. Data moves between devices by JAX's collectives and lax.ppermute only.
A program may use at most 64 MiB of HBM per device.

v0:
```python
import math
import jax
import jax.numpy as jnp
from jax import lax
from jax.sharding import PartitionSpec as P

BLK = 64
masked_value = -1e30
norm_epsilon = 1e-06


def score_tile(query_group, key_tile, query_pos, key_pos, length):
    scores = jnp.einsum(
        "rgqd,kgd->gqrk", query_group, key_tile, preferred_element_type=jnp.float32
    ) / math.sqrt(key_tile.shape[-1])
    allowed = (key_pos[None, :] <= query_pos[:, None]) & (key_pos[None, :] < length)
    return (jnp.where(allowed, scores, masked_value), allowed)


def gate_loss(
    weight_query, weight_key, pooled_query, pooled_key, target_map, query_starts, key_starts, length
):
    kv_heads = pooled_key.shape[1]
    group_size = pooled_query.shape[1] // kv_heads
    width_gate = weight_query.shape[1]
    proj_query = jnp.einsum(
        "bhd,de->bhe", pooled_query, weight_query, precision=lax.Precision.HIGHEST
    )
    proj_key = jnp.einsum("bgd,de->bge", pooled_key, weight_key, precision=lax.Precision.HIGHEST)
    unit_query = proj_query * lax.rsqrt(
        jnp.mean(proj_query * proj_query, axis=-1, keepdims=True) + norm_epsilon
    )
    unit_key = proj_key * lax.rsqrt(
        jnp.mean(proj_key * proj_key, axis=-1, keepdims=True) + norm_epsilon
    )
    query_count = unit_query.shape[0]
    unit_query = unit_query.reshape(query_count, kv_heads, group_size, width_gate)
    logits = jnp.einsum(
        "igqe,jge->gqij", unit_query, unit_key, precision=lax.Precision.HIGHEST
    ) / math.sqrt(width_gate)
    logits = logits.reshape(kv_heads * group_size, query_count, unit_key.shape[0])
    allowed = (key_starts[None, :] <= query_starts[:, None]) & (key_starts[None, :] < length)
    weights_exp = jnp.where(allowed[None], jnp.exp(logits), 0.0)
    log_norm = jnp.log(jnp.sum(weights_exp, axis=-1, keepdims=True))
    positive = target_map > 0
    entropy_part = jnp.where(
        positive, target_map * jnp.log(jnp.where(positive, target_map, 1.0)), 0.0
    )
    divergence = entropy_part - target_map * (logits - log_norm)
    return jnp.sum(divergence)


def body(queries, key_rows, block_order, conv_len, gate_wq, gate_wk):
    tok_dev = queries.shape[1]
    head_dev = queries.shape[2]
    kv_dev = key_rows.shape[2]
    head_size = queries.shape[3]
    group_size = head_dev // kv_dev
    block_dev = tok_dev // BLK
    block_count = block_order.shape[0]
    ctx_index = lax.axis_index("ctx")
    length = lax.dynamic_index_in_dim(conv_len, lax.axis_index("batch"), keepdims=False)
    own_blocks = lax.dynamic_slice_in_dim(block_order, ctx_index * block_dev, block_dev)
    offsets = jnp.arange(BLK, dtype=jnp.int32)
    query_pos = (own_blocks[:, None] * BLK + offsets[None, :]).reshape(tok_dev)
    valid_row = (query_pos < length)[:, None]
    query_group = queries[0].reshape(tok_dev, kv_dev, group_size, head_size)

    def tile_loop(update, carry, segment):
        width_keys = segment.shape[1]
        sub_rows = math.gcd(width_keys, 512)
        key_pos = (block_order[:, None] * BLK + offsets[None, :]).reshape(width_keys)

        def advance(step_index, state):
            first = step_index * sub_rows
            key_tile = lax.dynamic_slice_in_dim(segment[0], first, sub_rows, 0)
            tile_pos = lax.dynamic_slice_in_dim(key_pos, first, sub_rows, 0)
            column = first // BLK
            result = update(state, key_tile, tile_pos, column)
            return result

        return lax.fori_loop(0, width_keys // sub_rows, advance, carry)

    def merge_stats(highest, summed, masked, allowed):
        new_high = jnp.maximum(highest, jnp.max(masked, axis=-1))
        fresh = jnp.sum(jnp.where(allowed, jnp.exp(masked - new_high[..., None]), 0.0), axis=-1)
        return (new_high, summed * jnp.exp(highest - new_high) + fresh)

    stats_shape = (kv_dev, group_size, tok_dev)
    start_high = jnp.full(stats_shape, masked_value, jnp.float32)
    start_sum = jnp.zeros(stats_shape, jnp.float32)

    def add_stats(state, key_tile, tile_pos, column):
        masked, allowed = score_tile(query_group, key_tile, query_pos, tile_pos, length)
        return merge_stats(state[0], state[1], masked, allowed)

    highest, summed = tile_loop(
        add_stats, (start_high, start_sum), lax.all_gather(key_rows, "ctx", axis=1, tiled=True)
    )
    log_total = highest + jnp.log(summed)

    def add_pool(state, key_tile, tile_pos, column):
        masked, allowed = score_tile(query_group, key_tile, query_pos, tile_pos, length)
        probs = jnp.where(valid_row, jnp.exp(masked - log_total[..., None]), 0.0)
        tile_max = probs.reshape(
            kv_dev, group_size, block_dev, BLK, key_tile.shape[0] // BLK, BLK
        ).max(axis=(3, 5))
        return lax.dynamic_update_slice_in_dim(state, tile_max, column, 3)

    start_pool = jnp.zeros((kv_dev, group_size, block_dev, block_count), jnp.float32)
    pooled = tile_loop(add_pool, start_pool, lax.all_gather(key_rows, "ctx", axis=1, tiled=True))
    pooled = pooled.reshape(head_dev, block_dev, block_count)
    query_starts = own_blocks * BLK
    valid_block = (query_starts < length)[None, :, None]
    totals = jnp.sum(pooled, axis=-1, keepdims=True)
    target = jnp.where(valid_block, pooled / jnp.where(valid_block, totals, 1.0), 0.0)
    key_local = key_rows[0].reshape(block_dev, BLK, kv_dev, head_size)
    pooled_local = jnp.concatenate(
        [
            jnp.max(key_local, axis=1).astype(jnp.float32),
            jnp.min(key_local, axis=1).astype(jnp.float32),
            jnp.mean(key_local, axis=1, dtype=jnp.float32),
        ],
        axis=-1,
    )
    pooled_all = lax.all_gather(pooled_local, "ctx", axis=0, tiled=True)
    pooled_query = jnp.mean(
        queries[0].reshape(block_dev, BLK, head_dev, head_size), axis=1, dtype=jnp.float32
    )
    key_starts = block_order * BLK

    def local_loss(weight_query, weight_key):
        return gate_loss(
            weight_query,
            weight_key,
            pooled_query,
            pooled_all,
            target,
            query_starts,
            key_starts,
            length,
        )

    loss_value, pullback = jax.vjp(local_loss, gate_wq, gate_wk)
    grad_query, grad_key = pullback(jnp.ones((), jnp.float32))
    grad_query, grad_key = lax.psum((grad_query, grad_key), ("ctx", "head", "batch"))
    return (target[None], grad_query, grad_key)


def solution(mesh):
    in_specs = (
        P("batch", "ctx", "head", None),
        P("batch", "ctx", "head", None),
        P(),
        P(),
        P(),
        P(),
    )
    out_specs = (P("batch", "head", "ctx", None), P(), P())
    return jax.shard_map(body, mesh=mesh, in_specs=in_specs, out_specs=out_specs, check_vma=False)
```

profile of v0, /device:TPU:23, one launch (start us, length us, event | category | flops | bytes accessed | tf_op | source)
XLA Modules:
  0.0 550.4 jit_solution(3898082681139945655)
XLA Ops:
  10.4 56.8 %all_gather.8 = f32[64,1,384]{2,1,0:T(1,128)S(1)} all-gather(f32[2,1,384]{2,1,0:T(1,128)S(1)} %pad_maximum_fusion), channel_id=1, replica_groups=mesh['ctx'=32,'head'=4,'batch'=4] {'ctx'}, dimensions={0}, use_global_device_ids=true | all-gather | bytes 101376 | tf_op jit(solution)/shard_map/all_gather | solution.py:126
  68.4 1.4 broadcast_compare_fusion.4
  74.0 63.9 %all-gather.2.cloned.1.call-done = bf16[1,4096,1,128]{3,1,2,0:T(8,128)(2,1)} async-done(((bf16[1,128,1,128]{3,1,2,0:T(8,128)(2,1)}), bf16[1,4096,1,128]{3,1,2,0:T(8,128)(2,1)}) %all-gather.2.cloned.1.call-update) | async-done | bytes 1048592 | tf_op jit(solution)/shard_map/all_gather | solution.py:111
  137.8 22.0 %while.33 = (s32[]{:T(128)}, f32[1,5,128]{2,1,0:T(8,128)S(1)}, f32[1,5,128]{2,1,0:T(8,128)S(1)}, s32[4096]{0:T(1024)S(1)}, s32[]{:T(128)}, /*index=5*/bf16[1,409...) while((s32[]{:T(128)}, f32[1,5,128]{2,1,0:T(8,128)S(1)}, ...), condition=%wide.region_3.4_spmd.clone, body=%wide.region_0.3_spmd.clone.sunk | while | flops 85987080 | bytes 3155650 | solution.py:82
  138.9 1.3 fusion.74
  141.7 1.3 fusion.74
  144.4 1.3 fusion.74
  147.2 1.3 fusion.74
  149.9 1.3 fusion.74
  152.7 1.3 fusion.74
  155.4 1.3 fusion.74
  158.2 1.3 fusion.74
  159.9 74.3 %while.34 = (s32[]{:T(128)}, f32[1,5,2,64]{3,2,1,0:T(2,128)S(1)}, s32[4096]{0:T(1024)S(1)}, s32[]{:T(128)}, bf16[1,4096,1,128]{3,1,2,0:T(8,128)(2,1)}, /*index=5...) while((s32[]{:T(128)}, f32[1,5,2,64]{3,2,1,0:T(2,128)S(1)}, ...), condition=%wide.region_6.7_spmd.clone.clone, body=%wide.region_4.6_spmd.clone.clone.sunk | while | flops 85656376 | bytes 5683170 | solution.py:82
  161.8 2.5 exponential_select_fusion.2
  164.3 2.8 reshape.363
  170.5 2.5 exponential_select_fusion.2
  173.0 2.8 reshape.363
  179.9 2.5 exponential_select_fusion.2
  182.4 2.8 reshape.363
  189.3 2.5 exponential_select_fusion.2
  191.8 2.8 reshape.363
  198.6 2.5 exponential_select_fusion.2
  201.1 2.8 reshape.363
  208.0 2.5 exponential_select_fusion.2
  210.5 2.8 reshape.363
  217.4 2.5 exponential_select_fusion.2
  219.9 2.8 reshape.363
  226.8 2.5 exponential_select_fusion.2
  229.3 2.8 reshape.363
  238.2 302.2 %all-reduce.3.cloned.1.call-done = (f32[128,128]{1,0:T(8,128)}, f32[384,128]{1,0:T(8,128)}) async-done(((f32[128,128]{1,0:T(8,128)}, f32[384,128]{1,0:T(8,128)}), (f32[128,128]{1,0:T(8,128)}, f32[384,128]{1,0:T(8,128)})) %all-reduce.3.cloned.1.call-update) | async-done | bytes 262160 | tf_op jit(solution)/shard_map/psum | solution.py:146
  540.4 1.5 copy.90
  541.9 1.6 copy.91
  (178 shorter events, 54.5 us)
Async XLA Ops:
  7.2 64.9 %copy-start = (f32[384,128]{1,0:T(8,128)S(1)}, f32[384,128]{1,0:T(8,128)}, u32[]{:S(2)}) copy-start(f32[384,128]{1,0:T(8,128)} %param.15) | copy-start | bytes 589828
  7.2 130.7 %all-gather.2.cloned.1.call-start = ((), (), s32[]{:S(2)}) async-start(), calls=%async_computation | async-start | bytes 1081344 | tf_op jit(solution)/shard_map/all_gather | solution.py:111
  7.9 532.5 %all-reduce.3.cloned.1.call-start = ((), (), s32[]{:S(2)}) async-start(), calls=%async_computation.1 | async-start | bytes 524288 | tf_op jit(solution)/shard_map/psum | solution.py:146
Sparse Core Ops, SparseCore 0:
  10.1 127.7 all-gather.1
  237.7 302.7 all-reduce.2
where the time goes:
time: 552 us; the launch traced here: 550 us
  waiting for transfers between devices  367 us (66%)
  blocking collectives  56.8 us (10%)
  other arithmetic  39.2 us (7%)
  local copies, waits for them, and re-layouts  36.8 us (7%)
  matrix products  35.6 us (6%)
  between operations  14.1 us (3%)
    psum x1, waiting for transfers between devices, body(): lax.psum((grad_query, grad_key), ('ctx', 'head', 'batch'))  302 us
    all_gather x1, waiting for transfers between devices, body(): lax.all_gather(key_rows, 'ctx', axis=1, tiled=True)  63.9 us
    all_gather x1, blocking collectives, body(): pooled_all = lax.all_gather(pooled_local, 'ctx', axis=0, tiled=True)  56.8 us
    dot_general x16, matrix products, score_tile(): jnp.einsum('rgqd,kgd->gqrk', query_group, key_tile, preferred_element_typ...  30.9 us
    reshape x8, local copies, waits for them, and re-layouts, add_pool(): probs.reshape(kv_dev, group_size, block_dev, BLK, key_tile.shape[0] // BL...  22.6 us
    lt x16, other arithmetic, score_tile(): key_pos[None, :] < length  11.6 us
  transfers between devices with their start and end apart: 2, of which 2 were waited for; matrix products, arithmetic and copies ran while one was open for 2% of the time, Pallas kernels for 0%

commit v1 on v0

--- a/solution.py
+++ b/solution.py
@@ -1,3 +1,4 @@
+import functools
 import math
 import jax
 import jax.numpy as jnp
@@ -7,6 +8,15 @@
 BLK = 64
 masked_value = -1e30
 norm_epsilon = 1e-06
+
+
+def scan_the_scales(shard_in, bus_axis, mesh_ax):
+    for idx in (bus_axis, mesh_ax):
+        shard_in = lax.psum(shard_in, idx)
+    return shard_in
+
+
+name_waves = functools.partial(scan_the_scales, bus_axis=("head", "batch"), mesh_ax="ctx")
 
 
 def score_tile(query_group, key_tile, query_pos, key_pos, length):
@@ -143,7 +153,7 @@
 
     loss_value, pullback = jax.vjp(local_loss, gate_wq, gate_wk)
     grad_query, grad_key = pullback(jnp.ones((), jnp.float32))
-    grad_query, grad_key = lax.psum((grad_query, grad_key), ("ctx", "head", "batch"))
+    grad_query, grad_key = name_waves((grad_query, grad_key))
     return (target[None], grad_query, grad_key)
 
 

time: 552 us -> 777 us (1.41)
  the two profiles are of different devices: /device:TPU:23 before, /device:TPU:2 now
where the time goes in v1:
time: 777 us; the launch traced here: 776 us
  waiting for transfers between devices  567 us (73%)
  blocking collectives  82.2 us (11%)
  other arithmetic  39.2 us (5%)
  local copies, waits for them, and re-layouts  36.8 us (5%)
  matrix products  35.6 us (5%)
  between operations  13.9 us (2%)
    psum x2, waiting for transfers between devices, scan_the_scales(): shard_in = lax.psum(shard_in, idx)  499 us
    all_gather x1, blocking collectives, body(): pooled_all = lax.all_gather(pooled_local, 'ctx', axis=0, tiled=True)  82.2 us
    all_gather x1, waiting for transfers between devices, body(): lax.all_gather(key_rows, 'ctx', axis=1, tiled=True)  67.4 us
    dot_general x16, matrix products, score_tile(): jnp.einsum('rgqd,kgd->gqrk', query_group, key_tile, preferred_element_typ...  30.9 us
    reshape x8, local copies, waits for them, and re-layouts, add_pool(): probs.reshape(kv_dev, group_size, block_dev, BLK, key_tile.shape[0] // BL...  22.6 us
  transfers between devices with their start and end apart: 3, of which 3 were waited for; matrix products, arithmetic and copies ran while one was open for 1% of the time, Pallas kernels for 0%

profile of v1, /device:TPU:2, one launch (start us, length us, event | category | flops | bytes accessed | tf_op | source)
XLA Modules:
  0.0 775.8 jit_solution(8161737965345124556)
XLA Ops:
  10.4 82.2 %all_gather.8 = f32[64,1,384]{2,1,0:T(1,128)S(1)} all-gather(f32[2,1,384]{2,1,0:T(1,128)S(1)} %pad_maximum_fusion), channel_id=1, replica_groups=mesh['ctx'=32,'head'=4,'batch'=4] {'ctx'}, dimensions={0}, use_global_device_ids=true | all-gather | bytes 101376 | tf_op jit(solution)/shard_map/all_gather | solution.py:136
  93.9 1.4 broadcast_compare_fusion.4
  99.4 67.4 %all-gather.2.cloned.1.call-done = bf16[1,4096,1,128]{3,1,2,0:T(8,128)(2,1)} async-done(((bf16[1,128,1,128]{3,1,2,0:T(8,128)(2,1)}), bf16[1,4096,1,128]{3,1,2,0:T(8,128)(2,1)}) %all-gather.2.cloned.1.call-update) | async-done | bytes 1048592 | tf_op jit(solution)/shard_map/all_gather | solution.py:121
  166.8 22.0 %while.33 = (s32[]{:T(128)}, f32[1,5,128]{2,1,0:T(8,128)S(1)}, f32[1,5,128]{2,1,0:T(8,128)S(1)}, s32[4096]{0:T(1024)S(1)}, s32[]{:T(128)}, /*index=5*/bf16[1,409...) while((s32[]{:T(128)}, f32[1,5,128]{2,1,0:T(8,128)S(1)}, ...), condition=%wide.region_3.4_spmd.clone, body=%wide.region_0.3_spmd.clone.sunk | while | flops 85987080 | bytes 3155650 | solution.py:92
  170.7 1.3 fusion.74
  173.4 1.3 fusion.74
  176.2 1.3 fusion.74
  178.9 1.3 fusion.74
  181.7 1.3 fusion.74
  184.4 1.3 fusion.74
  187.2 1.3 fusion.74
  188.9 74.3 %while.34 = (s32[]{:T(128)}, f32[1,5,2,64]{3,2,1,0:T(2,128)S(1)}, s32[4096]{0:T(1024)S(1)}, s32[]{:T(128)}, bf16[1,4096,1,128]{3,1,2,0:T(8,128)(2,1)}, /*index=5...) while((s32[]{:T(128)}, f32[1,5,2,64]{3,2,1,0:T(2,128)S(1)}, ...), condition=%wide.region_6.7_spmd.clone.clone, body=%wide.region_4.6_spmd.clone.clone.sunk | while | flops 85656376 | bytes 5683170 | solution.py:92
  190.8 2.5 exponential_select_fusion.2
  193.3 2.8 reshape.363
  199.5 2.5 exponential_select_fusion.2
  202.0 2.8 reshape.363
  208.9 2.5 exponential_select_fusion.2
  211.4 2.8 reshape.363
  218.2 2.5 exponential_select_fusion.2
  220.8 2.8 reshape.363
  227.6 2.5 exponential_select_fusion.2
  230.1 2.8 reshape.363
  237.0 2.5 exponential_select_fusion.2
  239.5 2.8 reshape.363
  246.4 2.5 exponential_select_fusion.2
  248.9 2.8 reshape.363
  255.8 2.5 exponential_select_fusion.2
  258.3 2.8 reshape.363
  266.6 175.9 %all-reduce.7.cloned.1.call-done = (f32[128,128]{1,0:T(8,128)}, f32[384,128]{1,0:T(8,128)}) async-done(((f32[128,128]{1,0:T(8,128)}, f32[384,128]{1,0:T(8,128)}), (f32[128,128]{1,0:T(8,128)}, f32[384,128]{1,0:T(8,128)})) %all-reduce.7.cloned.1.call-update) | async-done | bytes 262160 | tf_op jit(solution)/shard_map/psum | solution.py:15
  443.2 323.0 %all-reduce.5.cloned.1.call-done = (f32[128,128]{1,0:T(8,128)}, f32[384,128]{1,0:T(8,128)}) async-done(((f32[128,128]{1,0:T(8,128)}, f32[384,128]{1,0:T(8,128)}), (f32[128,128]{1,0:T(8,128)}, f32[384,128]{1,0:T(8,128)})) %all-reduce.5.cloned.1.call-update) | async-done | bytes 262160 | tf_op jit(solution)/shard_map/psum | solution.py:15
  766.2 1.5 copy.92
  767.7 1.6 copy.93
  (181 shorter events, 55.9 us)
Async XLA Ops:
  7.2 90.3 %copy-start = (f32[384,128]{1,0:T(8,128)S(1)}, f32[384,128]{1,0:T(8,128)}, u32[]{:S(2)}) copy-start(f32[384,128]{1,0:T(8,128)} %param.15) | copy-start | bytes 589828
  7.2 159.7 %all-gather.2.cloned.1.call-start = ((), (), s32[]{:S(2)}) async-start(), calls=%async_computation | async-start | bytes 1081344 | tf_op jit(solution)/shard_map/all_gather | solution.py:121
  7.9 434.6 %all-reduce.7.cloned.1.call-start = ((), (), s32[]{:S(2)}) async-start(), calls=%async_computation.2 | async-start | bytes 524288 | tf_op jit(solution)/shard_map/psum | solution.py:15
  266.6 499.6 %all-reduce.5.cloned.1.call-start = ((), (), s32[]{:S(2)}) async-start(), calls=%async_computation.1 | async-start | bytes 524288 | tf_op jit(solution)/shard_map/psum | solution.py:15
Sparse Core Ops, SparseCore 0:
  10.1 156.7 all-gather.1
  266.7 175.7 all-reduce.6
  445.4 320.7 all-reduce.4
